TPU v7x, 128 devices: a whole 4x4x4 slice. The times are simulated.
128 devices in a mesh: gx: 8 (over z, x_lo), gy: 4 (over x_hi, core), ha: 4 (over y).
Axes of the slice: x: 4 (x_hi: 2, x_lo: 2; x = x_hi * 2 + x_lo), y: 4, z: 4, core: 2. Of those that a mesh axis runs over, the one named last changes fastest.
Arguments:
- tokens: bfloat16 [64, 64, 16, 384], P('gx', 'gy'), may hold values from -30 to 30
- input_weight: bfloat16 [384, 768], P(None, 'ha'), may hold values from -1 to 1
- output_weight: bfloat16 [256, 384], P('ha'), may hold values from -0.375 to 0.375
- tissue_bits: int32 [64, 64], P('gx', 'gy'), may hold values from 0 to 65535
- cotangent: bfloat16 [64, 64, 16, 384], P('gx', 'gy'), may hold values from -6 to 6
Outputs:
- token_gradient: bfloat16 [64, 64, 16, 384], P('gx', 'gy', None, 'ha')
- input_gradient: float32 [384, 768], P(None, 'ha')
- output_gradient: float32 [256, 384], P('ha')
All inputs are finite; a program needn't handle non-finite values.
Results may differ from a plain program's by a relative error of at most 0.018.
The roundings to bfloat16 on the way count: a program that leaves them out, or rounds other values in their place, can miss the bound.
Values may be sent and summed in bfloat16 or wider, within the bound.
No kernel may reach another device: no remote copies, remote signals or barrier semaphores. Data moves between devices by JAX's collectives and lax.ppermute only.
A program may use at most 128 MiB of HBM per device.

v0:
```python
import jax
import jax.numpy as jnp
from jax import lax
from jax.sharding import PartitionSpec as P

HD = 64
REACH = 3


def extended(block, sides, width):
    for axis, dim in sides:
        count = lax.axis_size(axis)
        forward = [(i, i + 1) for i in range(count - 1)]
        backward = [(target, source) for source, target in forward]
        low = lax.ppermute(
            lax.slice_in_dim(block, block.shape[dim] - width, None, axis=dim), axis, forward
        )
        high = lax.ppermute(lax.slice_in_dim(block, 0, width, axis=dim), axis, backward)
        block = jnp.concatenate([low, block, high], axis=dim)
    return block


def block_length(extent, plane_rows):
    for length in range(1, extent + 1):
        if extent % length == 0 and length * plane_rows >= 512:
            return length
    return extent


def shards(tokens, input_weight, output_weight, tissue_bits, cotangent):
    width_x, width_y, depth, model_width = tokens.shape
    local_heads = output_weight.shape[0] // HD
    token_count = width_x * width_y * depth
    score_scale = HD ** (-0.5)
    flat_tokens = tokens.reshape(token_count, model_width)
    flat_cotangent = cotangent.reshape(token_count, model_width)
    bit_values = 2 ** jnp.arange(depth, dtype=jnp.int32)
    key_valid = (tissue_bits[:, :, None] // bit_values % 2).astype(jnp.bfloat16)
    key_span_x_full = width_x + 2 * REACH
    key_span_y = width_y + 2 * REACH
    projected = jnp.dot(flat_tokens, input_weight, preferred_element_type=jnp.float32).astype(
        jnp.bfloat16
    )
    projected = projected.reshape(token_count, local_heads, 3, HD)
    queries = projected[:, :, 0, :].reshape(token_count, local_heads * HD)
    pair_local = projected[:, :, 1:, :].reshape(width_x, width_y, depth, local_heads * 2 * HD)
    pair_padded, valid_padded = (
        extended(pair_local, (("gx", 0), ("gy", 1)), REACH),
        extended(key_valid, (("gx", 0), ("gy", 1)), REACH),
    )
    upstream = jnp.einsum(
        "nd,ed->ne", flat_cotangent, output_weight, preferred_element_type=jnp.float32
    ).astype(jnp.bfloat16)
    block_x = block_length(width_x, width_y * depth)
    block_count = width_x // block_x
    key_span_x = block_x + 2 * REACH
    query_rows = block_x * width_y * depth
    key_rows = key_span_x * key_span_y * depth
    query_slots = jnp.arange(query_rows)
    query_x = query_slots // (width_y * depth)
    query_y = query_slots // depth % width_y
    query_z = query_slots % depth
    key_slots = jnp.arange(key_rows)
    key_x = key_slots // (key_span_y * depth) - REACH
    key_y = key_slots // depth % key_span_y - REACH
    key_z = key_slots % depth
    within = (
        (jnp.abs(query_x[:, None] - key_x[None, :]) <= REACH)
        & (jnp.abs(query_y[:, None] - key_y[None, :]) <= REACH)
        & (jnp.abs(query_z[:, None] - key_z[None, :]) <= REACH)
    )
    self_pair = (
        (query_x[:, None] == key_x[None, :])
        & (query_y[:, None] == key_y[None, :])
        & (query_z[:, None] == key_z[None, :])
    )
    query_grid = queries.reshape(width_x, width_y, depth, local_heads, HD)
    upstream_grid = upstream.reshape(width_x, width_y, depth, local_heads, HD)
    pair_grid = pair_padded.reshape(key_span_x_full, key_span_y, depth, local_heads, 2, HD)

    def attend_block(block_index, carry):
        query_sums, pair_sums, outputs = carry
        first_row = block_index * block_x
        query_block = lax.dynamic_slice_in_dim(query_grid, first_row, block_x, 0).reshape(
            query_rows, local_heads, HD
        )
        upstream_block = lax.dynamic_slice_in_dim(upstream_grid, first_row, block_x, 0).reshape(
            query_rows, local_heads, HD
        )
        pair_block = lax.dynamic_slice_in_dim(pair_grid, first_row, key_span_x, 0).reshape(
            key_rows, local_heads, 2, HD
        )
        keys_block = pair_block[:, :, 0, :]
        values_block = pair_block[:, :, 1, :]
        live_keys = (
            lax.dynamic_slice_in_dim(valid_padded, first_row, key_span_x, 0).reshape(key_rows) > 0
        )
        allowed = within & (live_keys[None, :] | self_pair)
        scores = (
            jnp.einsum("qhe,khe->hqk", query_block, keys_block, preferred_element_type=jnp.float32)
            * score_scale
        )
        scores = jnp.where(allowed[None], scores, -jnp.inf)
        row_max = jnp.max(scores, axis=-1, keepdims=True)
        raised = jnp.exp(scores - row_max)
        weights = (raised / jnp.sum(raised, axis=-1, keepdims=True)).astype(jnp.bfloat16)
        result = jnp.einsum(
            "hqk,khe->qhe", weights, values_block, preferred_element_type=jnp.float32
        )
        weight_gradient = jnp.einsum(
            "qhe,khe->hqk", upstream_block, values_block, preferred_element_type=jnp.float32
        )
        row_inner = jnp.sum(upstream_block.astype(jnp.float32) * result, axis=-1)
        score_gradient = (
            weights.astype(jnp.float32) * (weight_gradient - row_inner.T[:, :, None]) * score_scale
        ).astype(jnp.bfloat16)
        query_gradient = jnp.einsum(
            "hqk,khe->qhe", score_gradient, keys_block, preferred_element_type=jnp.float32
        )
        key_gradient = jnp.einsum(
            "hqk,qhe->khe", score_gradient, query_block, preferred_element_type=jnp.float32
        )
        value_gradient = jnp.einsum(
            "hqk,qhe->khe", weights, upstream_block, preferred_element_type=jnp.float32
        )
        pair_gradient = jnp.stack([key_gradient, value_gradient], axis=2).reshape(
            key_span_x, key_span_y, depth, local_heads * 2 * HD
        )
        query_sums = lax.dynamic_update_slice_in_dim(
            query_sums,
            query_gradient.reshape(block_x, width_y, depth, local_heads * HD),
            first_row,
            0,
        )
        previous = lax.dynamic_slice_in_dim(pair_sums, first_row, key_span_x, 0)
        pair_sums = lax.dynamic_update_slice_in_dim(
            pair_sums, previous + pair_gradient, first_row, 0
        )
        outputs = lax.dynamic_update_slice_in_dim(
            outputs,
            result.astype(jnp.bfloat16).reshape(block_x, width_y, depth, local_heads * HD),
            first_row,
            0,
        )
        return (query_sums, pair_sums, outputs)

    start = (
        jnp.zeros((width_x, width_y, depth, local_heads * HD), jnp.float32),
        jnp.zeros((key_span_x_full, key_span_y, depth, local_heads * 2 * HD), jnp.float32),
        jnp.zeros((width_x, width_y, depth, local_heads * HD), jnp.bfloat16),
    )
    query_sums, pair_sums, outputs = lax.fori_loop(0, block_count, attend_block, start)
    rims_first = jnp.concatenate([pair_sums[:REACH], pair_sums[width_x + REACH :]], axis=0)
    from_first = extended(rims_first.astype(jnp.bfloat16), (("gx", 0),), REACH).astype(
        rims_first.dtype
    )
    interior = pair_sums[REACH : width_x + REACH]
    interior = interior.at[:REACH].add(from_first[:REACH])
    interior = interior.at[width_x - REACH :].add(from_first[3 * REACH :])
    rims_second = jnp.concatenate([interior[:, :REACH], interior[:, width_y + REACH :]], axis=1)
    from_second = extended(rims_second.astype(jnp.bfloat16), (("gy", 1),), REACH).astype(
        rims_second.dtype
    )
    centre = interior[:, REACH : width_y + REACH]
    centre = centre.at[:, :REACH].add(from_second[:, :REACH])
    centre = centre.at[:, width_y - REACH :].add(from_second[:, 3 * REACH :])
    query_part = query_sums.reshape(token_count, local_heads, 1, HD)
    pair_part = centre.reshape(token_count, local_heads, 2, HD)
    dprojected = (
        jnp.concatenate([query_part, pair_part], axis=2)
        .reshape(token_count, local_heads * 3 * HD)
        .astype(jnp.bfloat16)
    )
    partial_terms = jnp.einsum(
        "nc,dc->nd", dprojected, input_weight, preferred_element_type=jnp.float32
    ).reshape(width_x, width_y, depth, model_width)
    token_gradient = lax.psum_scatter(partial_terms, "ha", scatter_dimension=3, tiled=True).astype(
        jnp.bfloat16
    )
    attended_flat = outputs.reshape(token_count, local_heads * HD)
    part_input = jnp.einsum(
        "nd,nc->dc", flat_tokens, dprojected, preferred_element_type=jnp.float32
    )
    part_output = jnp.einsum(
        "ne,nd->ed", attended_flat, flat_cotangent, preferred_element_type=jnp.float32
    )
    summed_input, summed_output = (
        lax.psum(part_input.astype(jnp.bfloat16), ("gx", "gy")).astype(jnp.float32),
        lax.psum(part_output.astype(jnp.bfloat16), ("gx", "gy")).astype(jnp.float32),
    )
    normaliser = (token_count * lax.axis_size("gx") * lax.axis_size("gy")) ** (-0.5)
    return (token_gradient, summed_input * normaliser, summed_output * normaliser)


def solution(mesh):
    placed = (
        P("gx", "gy", None, None),
        P(None, "ha"),
        P("ha", None),
        P("gx", "gy"),
        P("gx", "gy", None, None),
    )
    return jax.shard_map(
        shards,
        mesh=mesh,
        in_specs=placed,
        out_specs=(P("gx", "gy", None, "ha"), P(None, "ha"), P("ha", None)),
        check_vma=False,
    )
```

profile of v0, /device:TPU:0, one launch (start us, length us, event | category | flops | bytes accessed | tf_op | source)
XLA Modules:
  0.0 429.6 jit_solution(15858001204018962524)
XLA Ops:
  11.0 3.5 collective-permute-start.4
  24.8 5.9 %collective-permute-start = (bf16[3,16,16,128]{3,2,1,0:T(8,128)(2,1)}, bf16[3,16,16,128]{3,2,1,0:T(8,128)(2,1)}, u32[]{:S(2)}, u32[]{:S(2)}) collective-permute-start(bf16[3,16,16,128]{3,2,1,0:T(8,128)(2,1)} %slice.209), channel_id=1, source_target_pairs={{0,16},{16,32},{32,48},{48,64},{64,80},{80,96},{96,112},{1,17},{17... | collective-permute-start | bytes 589832 | tf_op jit(solution)/shard_map/ppermute | solution.py:15
  41.4 6.2 %collective-permute-start.2 = (bf16[14,3,16,128]{3,2,1,0:T(8,128)(2,1)S(1)}, bf16[14,3,16,128]{3,2,1,0:T(8,128)(2,1)S(1)}, u32[]{:S(2)}, u32[]{:S(2)}) collective-permute-start(bf16[14,3,16,128]{3,2,1,0:T(8,128)(2,1)S(1)} %get-tuple-element.401), channel_id=1, source_target_pairs={{0,4},{4,8},{8,12},{1,5},{5,9},{9,13},{2,6},{6,10},{10,14},{3,7},{... | collective-permute-start | bytes 516104 | tf_op jit(solution)/shard_map/ppermute | solution.py:15
  60.7 128.2 %while.23 = (s32[]{:T(128)}, bf16[8,16,16,64]{3,2,1,0:T(8,128)(2,1)}, f32[14,22,16,128]{3,2,1,0:T(8,128)}, bf16[8,16,16,64]{3,2,1,0:T(8,128)(2,1)}, bf16[14,22,1...) while((s32[]{:T(128)}, ...), condition=%wide.region_4.5_spmd.clone.clone, body=%wide.region_0.4_spmd.clone.clone.sunk | while | flops 1152845056 | bytes 82846784 | solution.py:152
  66.3 5.8 %fusion.85 = (f32[512]{0:T(512)S(1)}, f32[512,2816]{1,0:T(8,128)S(1)}) fusion(bf16[512,64]{1,0:T(8,128)(2,1)S(1)} %bitcast.150, bf16[2816,1,2,64]{3,0,2,1:T(8,128)(2,1)S(1)} %bitcast.143, pred[2816]{0:T(1024)(128)(4,1)S(1)} %gt.22, s32[2816]{0:T(1024)S(1)} %get-tuple-element.564, s32[512]{0:T(512)S(1)} %get-tuple-element.565, ...), kind=kOutput, calls=%fused_computation.123.clone.1 | convolution fusion | flops 214826496 | bytes 6667264 | tf_op jit(solution)/shard_map/while/body/eval_jaxpr/qhe,khe->hqk/dot_general | solution.py:100
  83.6 3.3 copy.74
  86.9 3.2 reshape.514
  98.4 5.8 %fusion.85 = (f32[512]{0:T(512)S(1)}, f32[512,2816]{1,0:T(8,128)S(1)}) fusion(bf16[512,64]{1,0:T(8,128)(2,1)S(1)} %bitcast.150, bf16[2816,1,2,64]{3,0,2,1:T(8,128)(2,1)S(1)} %bitcast.143, pred[2816]{0:T(1024)(128)(4,1)S(1)} %gt.22, s32[2816]{0:T(1024)S(1)} %get-tuple-element.564, s32[512]{0:T(512)S(1)} %get-tuple-element.565, ...), kind=kOutput, calls=%fused_computation.123.clone.1 | convolution fusion | flops 214826496 | bytes 6667264 | tf_op jit(solution)/shard_map/while/body/eval_jaxpr/qhe,khe->hqk/dot_general | solution.py:100
  115.7 3.3 copy.74
  119.0 3.2 reshape.514
  130.4 5.8 %fusion.85 = (f32[512]{0:T(512)S(1)}, f32[512,2816]{1,0:T(8,128)S(1)}) fusion(bf16[512,64]{1,0:T(8,128)(2,1)S(1)} %bitcast.150, bf16[2816,1,2,64]{3,0,2,1:T(8,128)(2,1)S(1)} %bitcast.143, pred[2816]{0:T(1024)(128)(4,1)S(1)} %gt.22, s32[2816]{0:T(1024)S(1)} %get-tuple-element.564, s32[512]{0:T(512)S(1)} %get-tuple-element.565, ...), kind=kOutput, calls=%fused_computation.123.clone.1 | convolution fusion | flops 214826496 | bytes 6667264 | tf_op jit(solution)/shard_map/while/body/eval_jaxpr/qhe,khe->hqk/dot_general | solution.py:100
  147.8 3.3 copy.74
  151.0 3.2 reshape.514
  162.5 5.8 %fusion.85 = (f32[512]{0:T(512)S(1)}, f32[512,2816]{1,0:T(8,128)S(1)}) fusion(bf16[512,64]{1,0:T(8,128)(2,1)S(1)} %bitcast.150, bf16[2816,1,2,64]{3,0,2,1:T(8,128)(2,1)S(1)} %bitcast.143, pred[2816]{0:T(1024)(128)(4,1)S(1)} %gt.22, s32[2816]{0:T(1024)S(1)} %get-tuple-element.564, s32[512]{0:T(512)S(1)} %get-tuple-element.565, ...), kind=kOutput, calls=%fused_computation.123.clone.1 | convolution fusion | flops 214826496 | bytes 6667264 | tf_op jit(solution)/shard_map/while/body/eval_jaxpr/qhe,khe->hqk/dot_general | solution.py:100
  179.8 3.3 copy.74
  191.0 3.6 collective-permute-start.8
  198.5 7.3 %collective-permute-done.9 = bf16[3,22,16,128]{3,2,1,0:T(8,128)(2,1)S(1)} collective-permute-done((bf16[3,22,16,128]{3,2,1,0:T(8,128)(2,1)S(1)}, bf16[3,22,16,128]{3,2,1,0:T(8,128)(2,1)S(1)}, u32[]{:S(2)}, u32[]{:S(2)}) %collective-permute-start.9) | collective-permute-done | bytes 270368 | tf_op jit(solution)/shard_map/ppermute | solution.py:18
  206.8 6.8 %collective-permute-start.10 = (bf16[8,3,16,128]{3,2,1,0:T(8,128)(2,1)}, bf16[8,3,16,128]{3,2,1,0:T(8,128)(2,1)}, u32[]{:S(2)}, u32[]{:S(2)}) collective-permute-start(bf16[8,3,16,128]{3,2,1,0:T(8,128)(2,1)} %get-tuple-element.405), channel_id=1, source_target_pairs={{0,4},{4,8},{8,12},{1,5},{5,9},{9,13},{2,6},{6,10},{10,14},{3,7},{... | collective-permute-start | bytes 294920 | tf_op jit(solution)/shard_map/ppermute | solution.py:15
  230.4 4.1 convert_element_type.112
  236.9 20.4 %copy.58 = f32[8,16,16,384]{2,1,0,3:T(8,128)} copy(f32[8,16,16,384]{3,2,1,0:T(8,128)} %fusion.14) | data formatting | bytes 6291456
  257.2 21.8 %reshape.511 = f32[384,2048]{1,0:T(8,128)} reshape(f32[384,8,16,16]{3,2,1,0:T(8,128)} %bitcast.147) | data formatting | bytes 6291456
  281.9 128.5 %psum.15 = bf16[64,384]{1,0:T(8,128)(2,1)S(1)} all-reduce(bf16[64,384]{1,0:T(8,128)(2,1)S(1)} %fusion.9), channel_id=1, replica_groups=mesh['gx'=8,'gy'=4,'ha'=4] {'gx','gy'}, use_global_device_ids=true, to_apply=%region_7.8 | all-reduce | flops 24576 | bytes 98304 | tf_op jit(solution)/shard_map/psum | solution.py:189
  412.7 4.7 %reshape.512 = bf16[96,8,16,16]{3,2,1,0:T(8,128)(2,1)} reshape(f32[96,2048]{1,0:T(8,128)} %reduce-scatter.4.cloned.1.call-done) | data formatting | bytes 1179648
  417.4 4.8 %copy.59 = bf16[8,16,16,96]{3,2,1,0:T(8,128)(2,1)} copy(bf16[8,16,16,96]{2,1,0,3:T(8,128)(2,1)} %bitcast.154) | data formatting | bytes 786432
  (197 shorter events, 150.0 us)
Async XLA Ops:
  8.0 7.8 %copy-start = (bf16[8,16,16,384]{3,2,1,0:T(8,128)(2,1)S(1)}, bf16[8,16,16,384]{3,2,1,0:T(8,128)(2,1)}, u32[]{:S(2)}) copy-start(bf16[8,16,16,384]{3,2,1,0:T(8,128)(2,1)} %param.15) | copy-start | bytes 4718596
  8.0 403.1 %all-reduce.2.cloned.1.call-start = ((), (), s32[]{:S(2)}) async-start(), calls=%async_computation.1 | async-start | bytes 294912 | tf_op jit(solution)/shard_map/psum | solution.py:188
  10.3 5.4 %copy-start.11 = (bf16[8,16,16]{2,1,0:T(8,128)(2,1)}, bf16[8,16,16]{2,1,0:T(8,128)(2,1)S(1)}, u32[]{:S(2)}) copy-start(bf16[8,16,16]{2,1,0:T(8,128)(2,1)S(1)} %fusion.17) | copy-start | bytes 12292
  11.0 24.1 %collective-permute-start.4 = (bf16[3,16,16]{2,1,0:T(8,128)(2,1)}, bf16[3,16,16]{2,1,0:T(8,128)(2,1)S(1)}, u32[]{:S(2)}, u32[]{:S(2)}) collective-permute-start(bf16[3,16,16]{2,1,0:T(8,128)(2,1)} %get-tuple-element.409), channel_id=1, source_target_pairs={{0,16},{16,32},{32,48},{48,64},{64,80},{80,96},{96,112},{1,17},{17... | collective-permute-start | bytes 4616 | tf_op jit(solution)/shard_map/ppermute | solution.py:15
  14.5 20.6 %collective-permute-start.5 = (bf16[3,16,16]{2,1,0:T(8,128)(2,1)}, bf16[3,16,16]{2,1,0:T(8,128)(2,1)}, u32[]{:S(2)}, u32[]{:S(2)}) collective-permute-start(bf16[3,16,16]{2,1,0:T(8,128)(2,1)} %get-tuple-element.410), channel_id=1, source_target_pairs={{16,0},{32,16},{48,32},{64,48},{80,64},{96,80},{112,96},{17,1},{33... | collective-permute-start | bytes 4616 | tf_op jit(solution)/shard_map/ppermute | solution.py:18
  15.8 15.5 %copy-start.4 = (bf16[8,16,16,384]{3,2,1,0:T(8,128)(2,1)S(1)}, bf16[8,16,16,384]{3,2,1,0:T(8,128)(2,1)}, u32[]{:S(2)}) copy-start(bf16[8,16,16,384]{3,2,1,0:T(8,128)(2,1)} %param.19) | copy-start | bytes 4718596
  21.4 18.1 %collective-permute-start.1 = (bf16[3,16,16,128]{3,2,1,0:T(8,128)(2,1)}, bf16[3,16,16,128]{3,2,1,0:T(8,128)(2,1)}, u32[]{:S(2)}, u32[]{:S(2)}) collective-permute-start(bf16[3,16,16,128]{3,2,1,0:T(8,128)(2,1)} %slice.212), channel_id=1, source_target_pairs={{16,0},{32,16},{48,32},{64,48},{80,64},{96,80},{112,96},{17,1},{33... | collective-permute-start | bytes 589832 | tf_op jit(solution)/shard_map/ppermute | solution.py:18
  24.8 13.6 %collective-permute-start = (bf16[3,16,16,128]{3,2,1,0:T(8,128)(2,1)}, bf16[3,16,16,128]{3,2,1,0:T(8,128)(2,1)}, u32[]{:S(2)}, u32[]{:S(2)}) collective-permute-start(bf16[3,16,16,128]{3,2,1,0:T(8,128)(2,1)} %slice.209), channel_id=1, source_target_pairs={{0,16},{16,32},{32,48},{48,64},{64,80},{80,96},{96,112},{1,17},{17... | collective-permute-start | bytes 589832 | tf_op jit(solution)/shard_map/ppermute | solution.py:15
  35.8 16.2 %collective-permute-start.6 = (bf16[14,3,16]{2,1,0:T(4,128)(2,1)S(1)}, bf16[14,3,16]{2,1,0:T(4,128)(2,1)S(1)}, u32[]{:S(2)}, u32[]{:S(2)}) collective-permute-start(bf16[14,3,16]{2,1,0:T(4,128)(2,1)S(1)} %get-tuple-element.407), channel_id=1, source_target_pairs={{0,4},{4,8},{8,12},{1,5},{5,9},{9,13},{2,6},{6,10},{10,14},{3,7},{... | collective-permute-start | bytes 4040 | tf_op jit(solution)/shard_map/ppermute | solution.py:15
  37.1 14.9 %collective-permute-start.7 = (bf16[14,3,16]{2,1,0:T(4,128)(2,1)S(1)}, bf16[14,3,16]{2,1,0:T(4,128)(2,1)S(1)}, u32[]{:S(2)}, u32[]{:S(2)}) collective-permute-start(bf16[14,3,16]{2,1,0:T(4,128)(2,1)S(1)} %get-tuple-element.408), channel_id=1, source_target_pairs={{4,0},{8,4},{12,8},{5,1},{9,5},{13,9},{6,2},{10,6},{14,10},{7,3},{... | collective-permute-start | bytes 4040 | tf_op jit(solution)/shard_map/ppermute | solution.py:18
  41.4 12.0 %collective-permute-start.2 = (bf16[14,3,16,128]{3,2,1,0:T(8,128)(2,1)S(1)}, bf16[14,3,16,128]{3,2,1,0:T(8,128)(2,1)S(1)}, u32[]{:S(2)}, u32[]{:S(2)}) collective-permute-start(bf16[14,3,16,128]{3,2,1,0:T(8,128)(2,1)S(1)} %get-tuple-element.401), channel_id=1, source_target_pairs={{0,4},{4,8},{8,12},{1,5},{5,9},{9,13},{2,6},{6,10},{10,14},{3,7},{... | collective-permute-start | bytes 516104 | tf_op jit(solution)/shard_map/ppermute | solution.py:15
  47.5 6.2 %collective-permute-start.3 = (bf16[14,3,16,128]{3,2,1,0:T(8,128)(2,1)S(1)}, bf16[14,3,16,128]{3,2,1,0:T(8,128)(2,1)}, u32[]{:S(2)}, u32[]{:S(2)}) collective-permute-start(bf16[14,3,16,128]{3,2,1,0:T(8,128)(2,1)S(1)} %get-tuple-element.402), channel_id=1, source_target_pairs={{4,0},{8,4},{12,8},{5,1},{9,5},{13,9},{6,2},{10,6},{14,10},{7,3},{... | collective-permute-start | bytes 516104 | tf_op jit(solution)/shard_map/ppermute | solution.py:18
  57.2 3.5 copy-start.13
  77.2 2.7 copy-start.2
  109.3 2.7 copy-start.2
  188.9 7.0 %copy-start.3 = (f32[14,22,16,128]{3,2,1,0:T(8,128)S(1)}, f32[14,22,16,128]{3,2,1,0:T(8,128)}, u32[]{:S(2)}) copy-start(f32[14,22,16,128]{3,2,1,0:T(8,128)} %get-tuple-element.223) | copy-start | bytes 7569412
  191.0 7.5 %collective-permute-start.8 = (bf16[3,22,16,128]{3,2,1,0:T(8,128)(2,1)S(1)}, bf16[3,22,16,128]{3,2,1,0:T(8,128)(2,1)S(1)}, u32[]{:S(2)}, u32[]{:S(2)}) collective-permute-start(bf16[3,22,16,128]{3,2,1,0:T(8,128)(2,1)S(1)} %get-tuple-element.399), channel_id=1, source_target_pairs={{0,16},{16,32},{32,48},{48,64},{64,80},{80,96},{96,112},{1,17},{17... | collective-permute-start | bytes 811016 | tf_op jit(solution)/shard_map/ppermute | solution.py:15
  194.6 11.3 %collective-permute-start.9 = (bf16[3,22,16,128]{3,2,1,0:T(8,128)(2,1)S(1)}, bf16[3,22,16,128]{3,2,1,0:T(8,128)(2,1)S(1)}, u32[]{:S(2)}, u32[]{:S(2)}) collective-permute-start(bf16[3,22,16,128]{3,2,1,0:T(8,128)(2,1)S(1)} %get-tuple-element.400), channel_id=1, source_target_pairs={{16,0},{32,16},{48,32},{64,48},{80,64},{96,80},{112,96},{17,1},{33... | collective-permute-start | bytes 811016 | tf_op jit(solution)/shard_map/ppermute | solution.py:18
  205.9 9.0 %copy-start.8 = (bf16[8,16,16,64]{3,2,1,0:T(8,128)(2,1)S(1)}, bf16[8,16,16,64]{3,2,1,0:T(8,128)(2,1)}, u32[]{:S(2)}) copy-start(bf16[8,16,16,64]{3,2,1,0:T(8,128)(2,1)} %get-tuple-element.222) | copy-start | bytes 786436
  206.8 10.1 %collective-permute-start.10 = (bf16[8,3,16,128]{3,2,1,0:T(8,128)(2,1)}, bf16[8,3,16,128]{3,2,1,0:T(8,128)(2,1)}, u32[]{:S(2)}, u32[]{:S(2)}) collective-permute-start(bf16[8,3,16,128]{3,2,1,0:T(8,128)(2,1)} %get-tuple-element.405), channel_id=1, source_target_pairs={{0,4},{4,8},{8,12},{1,5},{5,9},{9,13},{2,6},{6,10},{10,14},{3,7},{... | collective-permute-start | bytes 294920 | tf_op jit(solution)/shard_map/ppermute | solution.py:15
  213.6 6.3 %collective-permute-start.11 = (bf16[8,3,16,128]{3,2,1,0:T(8,128)(2,1)}, bf16[8,3,16,128]{3,2,1,0:T(8,128)(2,1)}, u32[]{:S(2)}, u32[]{:S(2)}) collective-permute-start(bf16[8,3,16,128]{3,2,1,0:T(8,128)(2,1)} %get-tuple-element.406), channel_id=1, source_target_pairs={{4,0},{8,4},{12,8},{5,1},{9,5},{13,9},{6,2},{10,6},{14,10},{7,3},{... | collective-permute-start | bytes 294920 | tf_op jit(solution)/shard_map/ppermute | solution.py:18
  216.9 9.6 %copy-start.9 = (bf16[2048,1,1,64]{0,3,2,1:T(8,128)(2,1)S(1)}, bf16[2048,1,1,64]{0,3,2,1:T(8,128)(2,1)}, u32[]{:S(2)}) copy-start(bf16[2048,1,1,64]{0,3,2,1:T(8,128)(2,1)} %copy.53) | copy-start | bytes 786436
  229.1 5.4 %copy-start.10 = (bf16[384,192]{0,1:T(8,128)(2,1)S(1)}, bf16[384,192]{0,1:T(8,128)(2,1)}, u32[]{:S(2)}) copy-start(bf16[384,192]{0,1:T(8,128)(2,1)} %param.16) | copy-start | bytes 442372
  230.3 182.4 %reduce-scatter.4.cloned.1.call-start = ((), (), s32[]{:S(2)}) async-start(), calls=%async_computation.2 | async-start | bytes 3932160
  (10 other events, 17.2 us)
Sparse Core Ops, SparseCore 0:
  230.5 102.9 all-reduce.1
Sparse Core Ops, SparseCore 1:
  279.2 42.6 reduce-scatter.3
where the time goes:
time: 432 us; the launch traced here: 430 us
  local copies, waits for them, and re-layouts  141 us (33%)
  blocking collectives  129 us (30%)
  matrix products  57 us (13%)
  other arithmetic  38.5 us (9%)
  starting transfers between devices  35 us (8%)
  between operations  15.9 us (4%)
  waiting for transfers between devices  13.2 us (3%)
    psum x1, blocking collectives, shards(): lax.psum(part_output.astype(jnp.bfloat16), ('gx', 'gy')).astype(jnp.float32)  129 us
    unnamed x34, local copies, waits for them, and re-layouts  60.2 us
    ppermute x6, starting transfers between devices, extended(): lax.ppermute(lax.slice_in_dim(block, block.shape[dim] - width, None, axis...  27.2 us
    dot_general x4, matrix products, attend_block(): jnp.einsum('qhe,khe->hqk', query_block, keys_block, preferred_element_typ...  23.3 us
    another operation x4, local copies, waits for them, and re-layouts, attend_block(): jnp.stack([key_gradient, value_gradient], axis=2)  13.1 us
    reshape x4, local copies, waits for them, and re-layouts, attend_block(): jnp.stack([key_gradient, value_gradient], axis=2)  12.6 us
    dynamic_update_slice x4, other arithmetic, attend_block(): lax.dynamic_update_slice_in_dim(pair_sums, previous + pair_gradient, firs...  10.7 us
    ppermute x6, waiting for transfers between devices, extended(): lax.ppermute(lax.slice_in_dim(block, 0, width, axis=dim), axis, backward)  10.7 us
  transfers between devices with their start and end apart: 14, of which 4 were waited for; matrix products, arithmetic and copies ran while one was open for 17% of the time, Pallas kernels for 0%

commit v1 on v0

--- a/solution.py
+++ b/solution.py
@@ -186,7 +186,7 @@
     )
     summed_input, summed_output = (
         lax.psum(part_input.astype(jnp.bfloat16), ("gx", "gy")).astype(jnp.float32),
-        lax.psum(part_output.astype(jnp.bfloat16), ("gx", "gy")).astype(jnp.float32),
+        lax.psum(lax.psum(part_output.astype(jnp.bfloat16), "gx"), "gy").astype(jnp.float32),
     )
     normaliser = (token_count * lax.axis_size("gx") * lax.axis_size("gy")) ** (-0.5)
     return (token_gradient, summed_input * normaliser, summed_output * normaliser)

time: 432 us -> 357 us (0.83)
  blocking collectives: 129 us -> 47.4 us
    psum x1 -> x2, blocking collectives: 129 us -> 47.4 us  [the longest x1 32.6 us: shards(): lax.psum(part_output.astype(jnp.bfloat16), 'gx')]
  transfers between devices with their start and end apart: 14 -> 14, of which waited for: 4 -> 5; matrix products, arithmetic and copies ran while one was open for 17% -> 21% of each run, Pallas kernels for 0% -> 0%
where the time goes in v1:
time: 357 us; the launch traced here: 352 us
  local copies, waits for them, and re-layouts  141 us (39%)
  matrix products  57 us (16%)
  blocking collectives  47.4 us (13%)
  other arithmetic  38.4 us (11%)
  starting transfers between devices  35 us (10%)
  waiting for transfers between devices  16.7 us (5%)
  between operations  15.9 us (4%)
    unnamed x34, local copies, waits for them, and re-layouts  60.3 us
    psum x1, blocking collectives, shards(): lax.psum(part_output.astype(jnp.bfloat16), 'gx')  32.6 us
    ppermute x6, starting transfers between devices, extended(): lax.ppermute(lax.slice_in_dim(block, block.shape[dim] - width, None, axis...  27.2 us
    dot_general x4, matrix products, attend_block(): jnp.einsum('qhe,khe->hqk', query_block, keys_block, preferred_element_typ...  23.3 us
    psum x1, blocking collectives, shards(): lax.psum(lax.psum(part_output.astype(jnp.bfloat16), 'gx'), 'gy')  14.8 us
    another operation x4, local copies, waits for them, and re-layouts, attend_block(): jnp.stack([key_gradient, value_gradient], axis=2)  13.2 us
    reshape x4, local copies, waits for them, and re-layouts, attend_block(): jnp.stack([key_gradient, value_gradient], axis=2)  12.6 us
    ppermute x6, waiting for transfers between devices, extended(): lax.ppermute(lax.slice_in_dim(block, 0, width, axis=dim), axis, backward)  10.7 us
  transfers between devices with their start and end apart: 14, of which 5 were waited for; matrix products, arithmetic and copies ran while one was open for 21% of the time, Pallas kernels for 0%

profile of v1, /device:TPU:0, one launch (start us, length us, event | category | flops | bytes accessed | tf_op | source)
XLA Modules:
  0.0 352.1 jit_solution(9443819936808401283)
XLA Ops:
  11.0 3.5 collective-permute-start.4
  24.8 5.8 %collective-permute-start = (bf16[3,16,16,128]{3,2,1,0:T(8,128)(2,1)}, bf16[3,16,16,128]{3,2,1,0:T(8,128)(2,1)}, u32[]{:S(2)}, u32[]{:S(2)}) collective-permute-start(bf16[3,16,16,128]{3,2,1,0:T(8,128)(2,1)} %slice.209), channel_id=1, source_target_pairs={{0,16},{16,32},{32,48},{48,64},{64,80},{80,96},{96,112},{1,17},{17... | collective-permute-start | bytes 589832 | tf_op jit(solution)/shard_map/ppermute | solution.py:15
  41.4 6.2 %collective-permute-start.2 = (bf16[14,3,16,128]{3,2,1,0:T(8,128)(2,1)S(1)}, bf16[14,3,16,128]{3,2,1,0:T(8,128)(2,1)S(1)}, u32[]{:S(2)}, u32[]{:S(2)}) collective-permute-start(bf16[14,3,16,128]{3,2,1,0:T(8,128)(2,1)S(1)} %get-tuple-element.401), channel_id=1, source_target_pairs={{0,4},{4,8},{8,12},{1,5},{5,9},{9,13},{2,6},{6,10},{10,14},{3,7},{... | collective-permute-start | bytes 516104 | tf_op jit(solution)/shard_map/ppermute | solution.py:15
  60.7 128.3 %while.23 = (s32[]{:T(128)}, bf16[8,16,16,64]{3,2,1,0:T(8,128)(2,1)}, f32[14,22,16,128]{3,2,1,0:T(8,128)}, bf16[8,16,16,64]{3,2,1,0:T(8,128)(2,1)}, bf16[14,22,1...) while((s32[]{:T(128)}, ...), condition=%wide.region_4.5_spmd.clone.clone, body=%wide.region_0.4_spmd.clone.clone.sunk | while | flops 1152845056 | bytes 82846784 | solution.py:152
  66.3 5.8 %fusion.85 = (f32[512]{0:T(512)S(1)}, f32[512,2816]{1,0:T(8,128)S(1)}) fusion(bf16[512,64]{1,0:T(8,128)(2,1)S(1)} %bitcast.150, bf16[2816,1,2,64]{3,0,2,1:T(8,128)(2,1)S(1)} %bitcast.143, pred[2816]{0:T(1024)(128)(4,1)S(1)} %gt.22, s32[2816]{0:T(1024)S(1)} %get-tuple-element.564, s32[512]{0:T(512)S(1)} %get-tuple-element.565, ...), kind=kOutput, calls=%fused_computation.123.clone.1 | convolution fusion | flops 214826496 | bytes 6667264 | tf_op jit(solution)/shard_map/while/body/eval_jaxpr/qhe,khe->hqk/dot_general | solution.py:100
  83.7 3.3 copy.74
  87.0 3.2 reshape.514
  98.4 5.8 %fusion.85 = (f32[512]{0:T(512)S(1)}, f32[512,2816]{1,0:T(8,128)S(1)}) fusion(bf16[512,64]{1,0:T(8,128)(2,1)S(1)} %bitcast.150, bf16[2816,1,2,64]{3,0,2,1:T(8,128)(2,1)S(1)} %bitcast.143, pred[2816]{0:T(1024)(128)(4,1)S(1)} %gt.22, s32[2816]{0:T(1024)S(1)} %get-tuple-element.564, s32[512]{0:T(512)S(1)} %get-tuple-element.565, ...), kind=kOutput, calls=%fused_computation.123.clone.1 | convolution fusion | flops 214826496 | bytes 6667264 | tf_op jit(solution)/shard_map/while/body/eval_jaxpr/qhe,khe->hqk/dot_general | solution.py:100
  115.7 3.3 copy.74
  130.5 5.8 %fusion.85 = (f32[512]{0:T(512)S(1)}, f32[512,2816]{1,0:T(8,128)S(1)}) fusion(bf16[512,64]{1,0:T(8,128)(2,1)S(1)} %bitcast.150, bf16[2816,1,2,64]{3,0,2,1:T(8,128)(2,1)S(1)} %bitcast.143, pred[2816]{0:T(1024)(128)(4,1)S(1)} %gt.22, s32[2816]{0:T(1024)S(1)} %get-tuple-element.564, s32[512]{0:T(512)S(1)} %get-tuple-element.565, ...), kind=kOutput, calls=%fused_computation.123.clone.1 | convolution fusion | flops 214826496 | bytes 6667264 | tf_op jit(solution)/shard_map/while/body/eval_jaxpr/qhe,khe->hqk/dot_general | solution.py:100
  147.8 3.3 copy.74
  162.6 5.8 %fusion.85 = (f32[512]{0:T(512)S(1)}, f32[512,2816]{1,0:T(8,128)S(1)}) fusion(bf16[512,64]{1,0:T(8,128)(2,1)S(1)} %bitcast.150, bf16[2816,1,2,64]{3,0,2,1:T(8,128)(2,1)S(1)} %bitcast.143, pred[2816]{0:T(1024)(128)(4,1)S(1)} %gt.22, s32[2816]{0:T(1024)S(1)} %get-tuple-element.564, s32[512]{0:T(512)S(1)} %get-tuple-element.565, ...), kind=kOutput, calls=%fused_computation.123.clone.1 | convolution fusion | flops 214826496 | bytes 6667264 | tf_op jit(solution)/shard_map/while/body/eval_jaxpr/qhe,khe->hqk/dot_general | solution.py:100
  179.9 3.3 copy.74
  191.1 3.6 %collective-permute-start.8 = (bf16[3,22,16,128]{3,2,1,0:T(8,128)(2,1)S(1)}, bf16[3,22,16,128]{3,2,1,0:T(8,128)(2,1)S(1)}, u32[]{:S(2)}, u32[]{:S(2)}) collective-permute-start(bf16[3,22,16,128]{3,2,1,0:T(8,128)(2,1)S(1)} %get-tuple-element.399), channel_id=1, source_target_pairs={{0,16},{16,32},{32,48},{48,64},{64,80},{80,96},{96,112},{1,17},{17... | collective-permute-start | bytes 811016 | tf_op jit(solution)/shard_map/ppermute | solution.py:15
  198.6 7.3 %collective-permute-done.9 = bf16[3,22,16,128]{3,2,1,0:T(8,128)(2,1)S(1)} collective-permute-done((bf16[3,22,16,128]{3,2,1,0:T(8,128)(2,1)S(1)}, bf16[3,22,16,128]{3,2,1,0:T(8,128)(2,1)S(1)}, u32[]{:S(2)}, u32[]{:S(2)}) %collective-permute-start.9) | collective-permute-done | bytes 270368 | tf_op jit(solution)/shard_map/ppermute | solution.py:18
  207.0 6.8 %collective-permute-start.10 = (bf16[8,3,16,128]{3,2,1,0:T(8,128)(2,1)}, bf16[8,3,16,128]{3,2,1,0:T(8,128)(2,1)}, u32[]{:S(2)}, u32[]{:S(2)}) collective-permute-start(bf16[8,3,16,128]{3,2,1,0:T(8,128)(2,1)} %get-tuple-element.405), channel_id=1, source_target_pairs={{0,4},{4,8},{8,12},{1,5},{5,9},{9,13},{2,6},{6,10},{10,14},{3,7},{... | collective-permute-start | bytes 294920 | tf_op jit(solution)/shard_map/ppermute | solution.py:15
  230.5 4.1 %convert_element_type.112 = bf16[8,16,16,192]{3,2,1,0:T(8,128)(2,1)S(1)} reshape(bf16[2048,1,3,64]{3,2,0,1:T(4,128)(2,1)} %copy.55) | data formatting | bytes 1572864 | tf_op jit(solution)/shard_map/convert_element_type | solution.py:172
  237.0 20.4 %copy.58 = f32[8,16,16,384]{2,1,0,3:T(8,128)} copy(f32[8,16,16,384]{3,2,1,0:T(8,128)} %fusion.14) | data formatting | bytes 6291456
  257.4 21.8 %reshape.511 = f32[384,2048]{1,0:T(8,128)} reshape(f32[384,8,16,16]{3,2,1,0:T(8,128)} %bitcast.147) | data formatting | bytes 6291456
  282.0 32.6 %psum.22 = bf16[64,384]{1,0:T(8,128)(2,1)S(1)} all-reduce(bf16[64,384]{1,0:T(8,128)(2,1)S(1)} %fusion.9), channel_id=1, replica_groups=mesh['gx'=8,'gy'=4,'ha'=4] {'gx'}, use_global_device_ids=true, to_apply=%region_7.8 | all-reduce | flops 24576 | bytes 98304 | tf_op jit(solution)/shard_map/psum | solution.py:189
  314.7 14.8 %psum.23 = bf16[64,384]{1,0:T(8,128)(2,1)S(1)} all-reduce(bf16[64,384]{1,0:T(8,128)(2,1)S(1)} %psum.22), channel_id=1, replica_groups=mesh['gx'=8,'gy'=4,'ha'=4] {'gy'}, use_global_device_ids=true, to_apply=%region_8.9 | all-reduce | flops 24576 | bytes 98304 | tf_op jit(solution)/shard_map/psum | solution.py:189
  330.1 3.4 all-reduce.2.cloned.1.call-done
  335.2 4.7 %reshape.512 = bf16[96,8,16,16]{3,2,1,0:T(8,128)(2,1)} reshape(f32[96,2048]{1,0:T(8,128)} %reduce-scatter.4.cloned.1.call-done) | data formatting | bytes 1179648
  339.8 4.8 %copy.59 = bf16[8,16,16,96]{3,2,1,0:T(8,128)(2,1)} copy(bf16[8,16,16,96]{2,1,0,3:T(8,128)(2,1)} %bitcast.154) | data formatting | bytes 786432
  (198 shorter events, 156.4 us)
Async XLA Ops:
  8.0 7.8 %copy-start = (bf16[8,16,16,384]{3,2,1,0:T(8,128)(2,1)S(1)}, bf16[8,16,16,384]{3,2,1,0:T(8,128)(2,1)}, u32[]{:S(2)}) copy-start(bf16[8,16,16,384]{3,2,1,0:T(8,128)(2,1)} %param.15) | copy-start | bytes 4718596
  8.0 325.5 %all-reduce.2.cloned.1.call-start = ((), (), s32[]{:S(2)}) async-start(), calls=%async_computation.1 | async-start | bytes 294912 | tf_op jit(solution)/shard_map/psum | solution.py:188
  10.3 5.4 %copy-start.11 = (bf16[8,16,16]{2,1,0:T(8,128)(2,1)}, bf16[8,16,16]{2,1,0:T(8,128)(2,1)S(1)}, u32[]{:S(2)}) copy-start(bf16[8,16,16]{2,1,0:T(8,128)(2,1)S(1)} %fusion.17) | copy-start | bytes 12292
  11.0 24.1 %collective-permute-start.4 = (bf16[3,16,16]{2,1,0:T(8,128)(2,1)}, bf16[3,16,16]{2,1,0:T(8,128)(2,1)S(1)}, u32[]{:S(2)}, u32[]{:S(2)}) collective-permute-start(bf16[3,16,16]{2,1,0:T(8,128)(2,1)} %get-tuple-element.409), channel_id=1, source_target_pairs={{0,16},{16,32},{32,48},{48,64},{64,80},{80,96},{96,112},{1,17},{17... | collective-permute-start | bytes 4616 | tf_op jit(solution)/shard_map/ppermute | solution.py:15
  14.5 20.6 %collective-permute-start.5 = (bf16[3,16,16]{2,1,0:T(8,128)(2,1)}, bf16[3,16,16]{2,1,0:T(8,128)(2,1)}, u32[]{:S(2)}, u32[]{:S(2)}) collective-permute-start(bf16[3,16,16]{2,1,0:T(8,128)(2,1)} %get-tuple-element.410), channel_id=1, source_target_pairs={{16,0},{32,16},{48,32},{64,48},{80,64},{96,80},{112,96},{17,1},{33... | collective-permute-start | bytes 4616 | tf_op jit(solution)/shard_map/ppermute | solution.py:18
  15.8 15.5 %copy-start.4 = (bf16[8,16,16,384]{3,2,1,0:T(8,128)(2,1)S(1)}, bf16[8,16,16,384]{3,2,1,0:T(8,128)(2,1)}, u32[]{:S(2)}) copy-start(bf16[8,16,16,384]{3,2,1,0:T(8,128)(2,1)} %param.19) | copy-start | bytes 4718596
  21.4 18.1 %collective-permute-start.1 = (bf16[3,16,16,128]{3,2,1,0:T(8,128)(2,1)}, bf16[3,16,16,128]{3,2,1,0:T(8,128)(2,1)}, u32[]{:S(2)}, u32[]{:S(2)}) collective-permute-start(bf16[3,16,16,128]{3,2,1,0:T(8,128)(2,1)} %slice.212), channel_id=1, source_target_pairs={{16,0},{32,16},{48,32},{64,48},{80,64},{96,80},{112,96},{17,1},{33... | collective-permute-start | bytes 589832 | tf_op jit(solution)/shard_map/ppermute | solution.py:18
  24.8 13.6 %collective-permute-start = (bf16[3,16,16,128]{3,2,1,0:T(8,128)(2,1)}, bf16[3,16,16,128]{3,2,1,0:T(8,128)(2,1)}, u32[]{:S(2)}, u32[]{:S(2)}) collective-permute-start(bf16[3,16,16,128]{3,2,1,0:T(8,128)(2,1)} %slice.209), channel_id=1, source_target_pairs={{0,16},{16,32},{32,48},{48,64},{64,80},{80,96},{96,112},{1,17},{17... | collective-permute-start | bytes 589832 | tf_op jit(solution)/shard_map/ppermute | solution.py:15
  35.8 16.2 %collective-permute-start.6 = (bf16[14,3,16]{2,1,0:T(4,128)(2,1)S(1)}, bf16[14,3,16]{2,1,0:T(4,128)(2,1)S(1)}, u32[]{:S(2)}, u32[]{:S(2)}) collective-permute-start(bf16[14,3,16]{2,1,0:T(4,128)(2,1)S(1)} %get-tuple-element.407), channel_id=1, source_target_pairs={{0,4},{4,8},{8,12},{1,5},{5,9},{9,13},{2,6},{6,10},{10,14},{3,7},{... | collective-permute-start | bytes 4040 | tf_op jit(solution)/shard_map/ppermute | solution.py:15
  37.1 14.9 %collective-permute-start.7 = (bf16[14,3,16]{2,1,0:T(4,128)(2,1)S(1)}, bf16[14,3,16]{2,1,0:T(4,128)(2,1)S(1)}, u32[]{:S(2)}, u32[]{:S(2)}) collective-permute-start(bf16[14,3,16]{2,1,0:T(4,128)(2,1)S(1)} %get-tuple-element.408), channel_id=1, source_target_pairs={{4,0},{8,4},{12,8},{5,1},{9,5},{13,9},{6,2},{10,6},{14,10},{7,3},{... | collective-permute-start | bytes 4040 | tf_op jit(solution)/shard_map/ppermute | solution.py:18
  41.4 12.0 %collective-permute-start.2 = (bf16[14,3,16,128]{3,2,1,0:T(8,128)(2,1)S(1)}, bf16[14,3,16,128]{3,2,1,0:T(8,128)(2,1)S(1)}, u32[]{:S(2)}, u32[]{:S(2)}) collective-permute-start(bf16[14,3,16,128]{3,2,1,0:T(8,128)(2,1)S(1)} %get-tuple-element.401), channel_id=1, source_target_pairs={{0,4},{4,8},{8,12},{1,5},{5,9},{9,13},{2,6},{6,10},{10,14},{3,7},{... | collective-permute-start | bytes 516104 | tf_op jit(solution)/shard_map/ppermute | solution.py:15
  47.6 6.2 %collective-permute-start.3 = (bf16[14,3,16,128]{3,2,1,0:T(8,128)(2,1)S(1)}, bf16[14,3,16,128]{3,2,1,0:T(8,128)(2,1)}, u32[]{:S(2)}, u32[]{:S(2)}) collective-permute-start(bf16[14,3,16,128]{3,2,1,0:T(8,128)(2,1)S(1)} %get-tuple-element.402), channel_id=1, source_target_pairs={{4,0},{8,4},{12,8},{5,1},{9,5},{13,9},{6,2},{10,6},{14,10},{7,3},{... | collective-permute-start | bytes 516104 | tf_op jit(solution)/shard_map/ppermute | solution.py:18
  57.3 3.5 copy-start.13
  77.3 2.7 copy-start.2
  109.3 2.7 copy-start.2
  189.0 7.0 %copy-start.3 = (f32[14,22,16,128]{3,2,1,0:T(8,128)S(1)}, f32[14,22,16,128]{3,2,1,0:T(8,128)}, u32[]{:S(2)}) copy-start(f32[14,22,16,128]{3,2,1,0:T(8,128)} %get-tuple-element.223) | copy-start | bytes 7569412
  191.1 7.5 %collective-permute-start.8 = (bf16[3,22,16,128]{3,2,1,0:T(8,128)(2,1)S(1)}, bf16[3,22,16,128]{3,2,1,0:T(8,128)(2,1)S(1)}, u32[]{:S(2)}, u32[]{:S(2)}) collective-permute-start(bf16[3,22,16,128]{3,2,1,0:T(8,128)(2,1)S(1)} %get-tuple-element.399), channel_id=1, source_target_pairs={{0,16},{16,32},{32,48},{48,64},{64,80},{80,96},{96,112},{1,17},{17... | collective-permute-start | bytes 811016 | tf_op jit(solution)/shard_map/ppermute | solution.py:15
  194.7 11.3 %collective-permute-start.9 = (bf16[3,22,16,128]{3,2,1,0:T(8,128)(2,1)S(1)}, bf16[3,22,16,128]{3,2,1,0:T(8,128)(2,1)S(1)}, u32[]{:S(2)}, u32[]{:S(2)}) collective-permute-start(bf16[3,22,16,128]{3,2,1,0:T(8,128)(2,1)S(1)} %get-tuple-element.400), channel_id=1, source_target_pairs={{16,0},{32,16},{48,32},{64,48},{80,64},{96,80},{112,96},{17,1},{33... | collective-permute-start | bytes 811016 | tf_op jit(solution)/shard_map/ppermute | solution.py:18
  206.0 9.0 %copy-start.8 = (bf16[8,16,16,64]{3,2,1,0:T(8,128)(2,1)S(1)}, bf16[8,16,16,64]{3,2,1,0:T(8,128)(2,1)}, u32[]{:S(2)}) copy-start(bf16[8,16,16,64]{3,2,1,0:T(8,128)(2,1)} %get-tuple-element.222) | copy-start | bytes 786436
  207.0 10.1 %collective-permute-start.10 = (bf16[8,3,16,128]{3,2,1,0:T(8,128)(2,1)}, bf16[8,3,16,128]{3,2,1,0:T(8,128)(2,1)}, u32[]{:S(2)}, u32[]{:S(2)}) collective-permute-start(bf16[8,3,16,128]{3,2,1,0:T(8,128)(2,1)} %get-tuple-element.405), channel_id=1, source_target_pairs={{0,4},{4,8},{8,12},{1,5},{5,9},{9,13},{2,6},{6,10},{10,14},{3,7},{... | collective-permute-start | bytes 294920 | tf_op jit(solution)/shard_map/ppermute | solution.py:15
  213.7 6.3 %collective-permute-start.11 = (bf16[8,3,16,128]{3,2,1,0:T(8,128)(2,1)}, bf16[8,3,16,128]{3,2,1,0:T(8,128)(2,1)}, u32[]{:S(2)}, u32[]{:S(2)}) collective-permute-start(bf16[8,3,16,128]{3,2,1,0:T(8,128)(2,1)} %get-tuple-element.406), channel_id=1, source_target_pairs={{4,0},{8,4},{12,8},{5,1},{9,5},{13,9},{6,2},{10,6},{14,10},{7,3},{... | collective-permute-start | bytes 294920 | tf_op jit(solution)/shard_map/ppermute | solution.py:18
  217.0 9.6 %copy-start.9 = (bf16[2048,1,1,64]{0,3,2,1:T(8,128)(2,1)S(1)}, bf16[2048,1,1,64]{0,3,2,1:T(8,128)(2,1)}, u32[]{:S(2)}) copy-start(bf16[2048,1,1,64]{0,3,2,1:T(8,128)(2,1)} %copy.53) | copy-start | bytes 786436
  229.2 5.4 %copy-start.10 = (bf16[384,192]{0,1:T(8,128)(2,1)S(1)}, bf16[384,192]{0,1:T(8,128)(2,1)}, u32[]{:S(2)}) copy-start(bf16[384,192]{0,1:T(8,128)(2,1)} %param.16) | copy-start | bytes 442372
  230.5 104.7 %reduce-scatter.4.cloned.1.call-start = ((), (), s32[]{:S(2)}) async-start(), calls=%async_computation.2 | async-start | bytes 3932160
  (10 other events, 17.3 us)
Sparse Core Ops, SparseCore 0:
  230.6 102.9 all-reduce.1
Sparse Core Ops, SparseCore 1:
  279.3 42.7 reduce-scatter.3
